TPU v7x, 256 devices: a whole 4x4x8 slice. The times are simulated.
256 devices in a mesh: ctx: 2 (over core), head: 4 (over x), doc: 32 (over z, y).
Axes of the slice: x: 4, y: 4, z: 8, core: 2. Of those that a mesh axis runs over, the one named last changes fastest.
Arguments:
- queries: bfloat16 [32, 256, 8192], P('doc', 'ctx', 'head'), may hold values from -360 to 360
- keys: bfloat16 [32, 8192, 1024], P('doc', 'ctx', 'head'), may hold values from -6 to 6
- values: bfloat16 [32, 8192, 1024], P('doc', 'ctx', 'head'), may hold values from -6 to 6
- pattern: int32 [32, 2, 16], P('doc'), may hold values from 0 to 63, as said below
Outputs:
- attended: bfloat16 [32, 256, 8192], P('doc', 'ctx', 'head')
- gram: float32 [8192, 8192], P(('head', 'ctx'), 'doc')
Inputs may be any that keep to these rules, and one draw needn't show every extreme that they name: Each row pattern[d, b, :] lists 16 different block numbers; no context shard (blocks s * 32 to (s + 1) * 32 - 1) holds more than 12 of one row's blocks, and in every draw some row has exactly 12 of its blocks in one shard.
All inputs are finite; a program needn't handle non-finite values.
Results may differ from a plain program's by a relative error of at most 0.015.
Values may be sent and summed in bfloat16 or wider, within the bound.
No kernel may reach another device: no remote copies, remote signals or barrier semaphores. Data moves between devices by JAX's collectives and lax.ppermute only.
A program may use at most 128 MiB of HBM per device.

v0:
```python
import jax
import jax.numpy as jnp
from jax import lax
from jax.sharding import PartitionSpec as P

HEAD_SIZE = 128
BLOCK_TOKENS = 128
QB_DEV = 1
NKB_DEV = 32
GROUP = 8
CAP = 12
NEGATIVE = -1e30


def in_order(pieces, dim):
    pieces = jnp.moveaxis(pieces, 0, dim)
    lengths = pieces.shape
    return pieces.reshape(*lengths[:dim], lengths[dim] * lengths[dim + 1], *lengths[dim + 2 :])


def sent_to_all(value, axis):
    size = lax.axis_size(axis)
    return lax.all_to_all(
        jnp.broadcast_to(value[None], (size, *value.shape)), axis, 0, 0, tiled=True
    )


def collect(value, axis, dim):
    return in_order(sent_to_all(value, axis), dim)


def in_blocks(value, dim, size):
    lengths = value.shape
    pieces = value.reshape(*lengths[:dim], size, lengths[dim] // size, *lengths[dim + 1 :])
    return jnp.moveaxis(pieces, dim, 0)


def cut_rows(length, count):
    lap = length // count
    if lap >= 8:
        lap -= lap % 8
    return [lap * k for k in range(1, count)]


def several_exchanges(value, axis, pieces, split_dim, concat_dim):
    blocks = in_blocks(value, split_dim, lax.axis_size(axis))
    split_at = max(range(1, max(2, blocks.ndim - 1)), key=lambda d: blocks.shape[d])
    gathered = []
    for share in jnp.split(blocks, cut_rows(blocks.shape[split_at], pieces), axis=split_at):
        if share.size:
            gathered.append(lax.all_to_all(share, axis, split_axis=0, concat_axis=0, tiled=True))
    return in_order(jnp.concatenate(gathered, axis=split_at), concat_dim)


def owned_slots(pattern_rows, owner):
    mine = pattern_rows // NKB_DEV == owner
    order = jnp.argsort(1 - mine.astype(jnp.int32), axis=1, stable=True)[:, :CAP]
    picked = jnp.take_along_axis(pattern_rows, order, axis=1) % NKB_DEV
    valid = jnp.take_along_axis(mine, order, axis=1)
    return (picked, valid)


def attend_block(query, key_blocks, value_blocks, valid):
    slots = key_blocks.shape[0]
    kv_heads = key_blocks.shape[2] // HEAD_SIZE
    grouped = query.reshape(BLOCK_TOKENS, kv_heads, GROUP, HEAD_SIZE)
    key_row_list = key_blocks.reshape(slots * BLOCK_TOKENS, kv_heads, HEAD_SIZE)
    value_row_list = value_blocks.reshape(slots * BLOCK_TOKENS, kv_heads, HEAD_SIZE)
    scores = jnp.einsum(
        "qkgd,skd->kgqs", grouped, key_row_list, preferred_element_type=jnp.float32
    ) * HEAD_SIZE ** (-0.5)
    live = jnp.broadcast_to(valid[:, None], (slots, BLOCK_TOKENS)).reshape(slots * BLOCK_TOKENS)
    scores = jnp.where(live, scores, NEGATIVE)
    top = jnp.max(scores, axis=-1)
    weights = jnp.where(live, jnp.exp(scores - top[..., None]), 0.0)
    total = jnp.sum(weights, axis=-1)
    mixed = jnp.einsum(
        "kgqs,skd->qkgd",
        weights.astype(jnp.bfloat16),
        value_row_list,
        preferred_element_type=jnp.float32,
    )
    heads = kv_heads * GROUP
    top_rows = jnp.transpose(top, (2, 0, 1)).reshape(BLOCK_TOKENS, heads)
    total_rows = jnp.transpose(total, (2, 0, 1)).reshape(BLOCK_TOKENS, heads)
    return (mixed.reshape(BLOCK_TOKENS, heads, HEAD_SIZE), top_rows, total_rows)


def per_device(queries, keys, values, pattern):
    ctx_count = lax.axis_size("ctx")
    head_count = lax.axis_size("head")
    doc_count = lax.axis_size("doc")
    owner = lax.axis_index("ctx")
    tok_rows = queries.shape[1]
    width = queries.shape[2]
    key_blocks = keys[0].reshape(NKB_DEV, BLOCK_TOKENS, keys.shape[2])
    value_blocks = values[0].reshape(NKB_DEV, BLOCK_TOKENS, values.shape[2])
    picked, valid = owned_slots(pattern[0], owner)
    send_keys = key_blocks[picked].reshape(ctx_count, QB_DEV, CAP, BLOCK_TOKENS, keys.shape[2])
    send_values = value_blocks[picked].reshape(
        ctx_count, QB_DEV, CAP, BLOCK_TOKENS, values.shape[2]
    )
    got_keys, got_values = (
        lax.all_to_all(send_keys, "ctx", split_axis=0, concat_axis=0, tiled=True),
        lax.all_to_all(send_values, "ctx", split_axis=0, concat_axis=0, tiled=True),
    )
    got_keys = jnp.swapaxes(got_keys, 0, 1).reshape(
        QB_DEV, ctx_count * CAP, BLOCK_TOKENS, keys.shape[2]
    )
    got_values = jnp.swapaxes(got_values, 0, 1).reshape(
        QB_DEV, ctx_count * CAP, BLOCK_TOKENS, values.shape[2]
    )
    own_rows = lax.dynamic_slice_in_dim(pattern[0], owner * QB_DEV, QB_DEV, 0)
    sources = jnp.arange(ctx_count, dtype=jnp.int32)
    counts = jnp.sum(own_rows[:, :, None] // NKB_DEV == sources[None, None, :], axis=1)
    live = (jnp.arange(CAP)[None, None, :] < counts[:, :, None]).reshape(QB_DEV, ctx_count * CAP)
    query_block_list = queries[0].reshape(QB_DEV, BLOCK_TOKENS, width)

    def one_owned(items):
        query, key_set, value_set, ok = items
        return attend_block(query, key_set, value_set, ok)

    mixed, top, total = lax.map(one_owned, (query_block_list, got_keys, got_values, live))
    attended = (mixed / total[..., None]).astype(jnp.bfloat16).reshape(tok_rows, width)
    sub = width // ctx_count
    model_width = width * head_count
    span = collect(attended, "ctx", 0)
    mine_cols = lax.dynamic_slice_in_dim(span, owner * sub, sub, 1)
    full_doc = lax.all_gather(span, "head", axis=1, tiled=True)
    slice_width = model_width // doc_count
    split_cols = full_doc.reshape(tok_rows * ctx_count, doc_count, slice_width)
    column_set = several_exchanges(split_cols, "doc", 2, 1, 0).reshape(
        doc_count * tok_rows * ctx_count, slice_width
    )
    product = lax.dot_general(
        lax.all_gather(mine_cols, "doc", axis=0, tiled=True),
        column_set,
        (((0,), (0,)), ((), ())),
        preferred_element_type=jnp.float32,
    )
    return (attended.reshape(1, tok_rows, width), product)


def solution(mesh):
    placed = (
        P("doc", "ctx", "head"),
        P("doc", "ctx", "head"),
        P("doc", "ctx", "head"),
        P("doc", None, None),
    )
    return jax.shard_map(
        per_device,
        mesh=mesh,
        in_specs=placed,
        out_specs=(P("doc", "ctx", "head"), P(("head", "ctx"), "doc")),
        check_vma=False,
    )
```

profile of v0, /device:TPU:8, one launch (start us, length us, event | category | flops | bytes accessed | tf_op | source)
XLA Modules:
  0.0 352.8 jit_solution(10864204959958701672)
XLA Ops:
  9.0 1.5 gather_fusion.2
  10.9 1.9 gather_fusion.1
  12.8 3.8 %all-to-all-start.1 = ((bf16[2,1,12,128,256]{4,3,2,1,0:T(8,128)(2,1)}), bf16[2,1,12,128,256]{4,3,2,1,0:T(8,128)(2,1)S(1)}, u32[]{:S(2)}, u32[]{:S(2)}) async-start(bf16[2,1,12,128,256]{4,3,2,1,0:T(8,128)(2,1)} %bitcast.79), calls=%async_computation.1 | async-start | bytes 3145728 | tf_op jit(solution)/shard_map/all_to_all | solution.py:104
  17.2 3.4 gather_fusion
  20.7 4.7 %all-to-all-start = ((bf16[2,1,12,128,256]{4,3,2,1,0:T(8,128)(2,1)}), bf16[2,1,12,128,256]{4,3,2,1,0:T(8,128)(2,1)}, u32[]{:S(2)}, u32[]{:S(2)}) async-start(bf16[2,1,12,128,256]{4,3,2,1,0:T(8,128)(2,1)} %bitcast.80), calls=%async_computation | async-start | bytes 3145728 | tf_op jit(solution)/shard_map/all_to_all | solution.py:105
  25.4 1.9 reshape.226
  27.2 17.6 %fusion.33 = (f32[2,8,128]{2,1,0:T(8,128)S(1)}, bf16[2,8,128,3072]{2,3,1,0:T(8,128)(2,1)}) fusion(pred[3072]{0:T(1024)(128)(4,1)S(1)} %broadcast_bitcast_fusion, bf16[3072,2,128,1]{2,1,0,3:T(2,128)(2,1)} %bitcast.84, bf16[128,2,8,128]{3,2,1,0:T(8,128)(2,1)S(1)} %bitcast.87), kind=kOutput, calls=%fused_computation.58 | convolution fusion | flops 1648364544 | bytes 14691328 | tf_op jit(solution)/shard_map/while/body/eval_jaxpr/sub | solution.py:75
  44.8 3.5 reshape.223
  48.3 7.0 %fusion.6 = f32[2,128,8,128]{3,1,2,0:T(8,128)S(1)} fusion(bf16[2,8,128,3072]{2,3,1,0:T(8,128)(2,1)} %get-tuple-element.28, bf16[3072,2,128,1]{2,1,0,3:T(2,128)(2,1)} %bitcast.81), kind=kOutput, calls=%fused_computation.10 | convolution fusion | flops 1610612736 | bytes 15204352 | tf_op jit(solution)/shard_map/while/body/eval_jaxpr/kgqs,skd->qkgd/dot_general | solution.py:77
  55.5 4.6 %all_to_all.25 = bf16[2,128,2048]{1,2,0:T(8,128)(2,1)S(1)} all-to-all(bf16[2,128,2048]{1,2,0:T(8,128)(2,1)S(1)} %broadcast_in_dim.63), channel_id=1, replica_groups=mesh['ctx'=2,'head'=4,'doc'=32] {'ctx'}, dimensions={0} | all-to-all | bytes 2097152 | tf_op jit(solution)/shard_map/all_to_all | solution.py:23
  61.2 1.9 constant_dynamic-slice_fusion
  63.1 51.9 %all-gather.5.cloned.1.call-done = bf16[256,8192]{0,1:T(8,128)(2,1)} async-done(((bf16[256,2048]{0,1:T(8,128)(2,1)}), bf16[256,8192]{0,1:T(8,128)(2,1)}) %all-gather.5.cloned.1.call-update) | async-done | bytes 4194320 | tf_op jit(solution)/shard_map/all_gather | solution.py:129
  115.0 4.0 %slice_bitcast_fusion.1 = (bf16[32,128,1,256]{1,3,2,0:T(8,128)(2,1)S(1)}, bf16[32,128,1,256]{1,3,2,0:T(8,128)(2,1)}) fusion(bf16[32,256,1,256]{1,3,0,2:T(8,128)(2,1)} %bitcast.82), kind=kLoop, calls=%fused_computation.18 | loop fusion | bytes 8388608 | tf_op jit(solution)/shard_map/split | solution.py:49
  119.0 74.1 %all_to_all.26 = bf16[32,128,1,256]{1,3,2,0:T(8,128)(2,1)} all-to-all(bf16[32,128,1,256]{1,3,2,0:T(8,128)(2,1)S(1)} %get-tuple-element.18), channel_id=1, replica_groups=mesh['ctx'=2,'head'=4,'doc'=32] {'doc'}, dimensions={0} | all-to-all | bytes 4194304 | tf_op jit(solution)/shard_map/all_to_all | solution.py:51
  193.1 5.7 %all-to-all-start.4 = ((bf16[32,128,1,256]{1,3,2,0:T(8,128)(2,1)}), bf16[32,128,1,256]{1,3,2,0:T(8,128)(2,1)}, u32[]{:S(2)}, u32[]{:S(2)}) async-start(bf16[32,128,1,256]{1,3,2,0:T(8,128)(2,1)} %get-tuple-element.19), calls=%async_computation.4 | async-start | bytes 4194304 | tf_op jit(solution)/shard_map/all_to_all | solution.py:51
  199.2 1.3 div.59
  200.5 2.5 div.60
  203.1 2.2 divide_convert_fusion
  205.2 2.9 copy.80
  208.2 51.0 %all-to-all-done.4 = bf16[32,128,1,256]{1,3,2,0:T(8,128)(2,1)} async-done(((bf16[32,128,1,256]{1,3,2,0:T(8,128)(2,1)}), bf16[32,128,1,256]{1,3,2,0:T(8,128)(2,1)}, u32[]{:S(2)}, u32[]{:S(2)}) %all-to-all-start.4) | async-done | bytes 2097184 | tf_op jit(solution)/shard_map/all_to_all | solution.py:51
  259.2 4.1 %copy.81 = bf16[32,128,1,256]{3,1,0,2:T(8,128)(2,1)} copy(bf16[32,128,1,256]{1,3,2,0:T(8,128)(2,1)} %all-to-all-done.4) | data formatting | bytes 4194304 | tf_op jit(solution)/shard_map/all_to_all | solution.py:51
  263.3 4.0 %pad_maximum_fusion = bf16[32,256,1,256]{3,1,0,2:T(8,128)(2,1)} fusion(bf16[32,128,1,256]{3,1,0,2:T(8,128)(2,1)} %copy.81, bf16[32,128,1,256]{3,1,0,2:T(8,128)(2,1)S(1)} %copy-done.4), kind=kLoop, calls=%fused_computation.15 | loop fusion | flops 8388608 | bytes 8388608 | tf_op jit(solution)/shard_map/concatenate | solution.py:52
  267.3 66.1 %all-gather.3.cloned.1.call-done = bf16[8192,1024]{0,1:T(8,128)(2,1)} async-done(((bf16[256,1024]{0,1:T(8,128)(2,1)}), bf16[8192,1024]{0,1:T(8,128)(2,1)}) %all-gather.3.cloned.1.call-update) | async-done | bytes 16777232 | tf_op jit(solution)/shard_map/all_gather | solution.py:136
  333.3 12.6 %fusion.42 = f32[1024,256]{1,0:T(8,128)} fusion(bf16[8192,1024]{0,1:T(8,128)(2,1)} %all-gather.3.cloned.1.call-done, bf16[8192,256]{1,0:T(8,128)(2,1)} %bitcast.83), kind=kOutput, calls=%fused_computation.59 | convolution fusion | flops 4294967296 | bytes 22020096 | tf_op jit(solution)/shard_map/dot_general | solution.py:135
  (46 shorter events, 4.6 us)
Async XLA Ops:
  7.2 3.8 %copy-start = (bf16[1,4096,256]{2,1,0:T(8,128)(2,1)S(1)}, bf16[1,4096,256]{2,1,0:T(8,128)(2,1)}, u32[]{:S(2)}) copy-start(bf16[1,4096,256]{2,1,0:T(8,128)(2,1)} %param.5) | copy-start | bytes 6291460
  12.8 3.8 %copy-start.2 = (s32[1,2,16]{2,1,0:T(2,128)S(1)}, s32[1,2,16]{2,1,0:T(2,128)}, u32[]{:S(2)}) copy-start(s32[1,2,16]{2,1,0:T(2,128)} %param.7) | copy-start | bytes 388
  12.8 4.3 %copy-start.5 = (bf16[1,128,2048]{2,1,0:T(8,128)(2,1)S(1)}, bf16[1,128,2048]{2,1,0:T(8,128)(2,1)}, u32[]{:S(2)}) copy-start(bf16[1,128,2048]{2,1,0:T(8,128)(2,1)} %param.4) | copy-start | bytes 1572868
  12.8 7.9 %all-to-all-start.1 = ((bf16[2,1,12,128,256]{4,3,2,1,0:T(8,128)(2,1)}), bf16[2,1,12,128,256]{4,3,2,1,0:T(8,128)(2,1)S(1)}, u32[]{:S(2)}, u32[]{:S(2)}) async-start(bf16[2,1,12,128,256]{4,3,2,1,0:T(8,128)(2,1)} %bitcast.79), calls=%async_computation.1 | async-start | bytes 3145728 | tf_op jit(solution)/shard_map/all_to_all | solution.py:104
  20.7 24.1 %all-to-all-start = ((bf16[2,1,12,128,256]{4,3,2,1,0:T(8,128)(2,1)}), bf16[2,1,12,128,256]{4,3,2,1,0:T(8,128)(2,1)}, u32[]{:S(2)}, u32[]{:S(2)}) async-start(bf16[2,1,12,128,256]{4,3,2,1,0:T(8,128)(2,1)} %bitcast.80), calls=%async_computation | async-start | bytes 3145728 | tf_op jit(solution)/shard_map/all_to_all | solution.py:105
  25.3 89.7 %all-gather.5.cloned.1.call-start = ((), (), s32[]{:S(2)}) async-start(), calls=%async_computation.6 | async-start | bytes 5242880 | tf_op jit(solution)/shard_map/all_gather | solution.py:129
  61.2 272.2 %all-gather.3.cloned.1.call-start = ((), (), s32[]{:S(2)}) async-start(), calls=%async_computation.5 | async-start | bytes 17301504 | tf_op jit(solution)/shard_map/all_gather | solution.py:136
  193.1 66.0 %all-to-all-start.4 = ((bf16[32,128,1,256]{1,3,2,0:T(8,128)(2,1)}), bf16[32,128,1,256]{1,3,2,0:T(8,128)(2,1)}, u32[]{:S(2)}, u32[]{:S(2)}) async-start(bf16[32,128,1,256]{1,3,2,0:T(8,128)(2,1)} %get-tuple-element.19), calls=%async_computation.4 | async-start | bytes 4194304 | tf_op jit(solution)/shard_map/all_to_all | solution.py:51
  200.5 4.7 %copy-start.3 = (bf16[32,128,1,256]{1,3,2,0:T(8,128)(2,1)S(1)}, bf16[32,128,1,256]{1,3,2,0:T(8,128)(2,1)}, u32[]{:S(2)}) copy-start(bf16[32,128,1,256]{1,3,2,0:T(8,128)(2,1)} %all_to_all.26) | copy-start | bytes 6291460
  208.2 55.1 %copy-start.4 = (bf16[32,128,1,256]{3,1,0,2:T(8,128)(2,1)S(1)}, bf16[32,128,1,256]{3,1,0,2:T(8,128)(2,1)}, u32[]{:S(2)}) copy-start(bf16[32,128,1,256]{3,1,0,2:T(8,128)(2,1)} %copy.80) | copy-start | bytes 6291460
  333.3 12.6 %copy-start.1 = (bf16[1,4096,256]{2,1,0:T(8,128)(2,1)S(1)}, bf16[1,4096,256]{2,1,0:T(8,128)(2,1)}, u32[]{:S(2)}) copy-start(bf16[1,4096,256]{2,1,0:T(8,128)(2,1)} %param.5) | copy-start | bytes 6291460
Sparse Core Ops, SparseCore 0:
  61.3 53.6 all-gather.4
  117.5 215.8 all-gather.2
where the time goes:
time: 353 us
  waiting for transfers between devices  169 us (48%)
  blocking collectives  78.7 us (22%)
  matrix products  37.1 us (11%)
  local copies, waits for them, and re-layouts  32.5 us (9%)
  starting transfers between devices  14.2 us (4%)
  between operations  14.2 us (4%)
  other arithmetic  7.17 us (2%)
    all_to_all x1, blocking collectives, several_exchanges(): lax.all_to_all(share, axis, split_axis=0, concat_axis=0, tiled=True)  74.1 us
    all_gather x1, waiting for transfers between devices, per_device(): lax.all_gather(mine_cols, 'doc', axis=0, tiled=True)  66.1 us
    all_gather x1, waiting for transfers between devices, per_device(): full_doc = lax.all_gather(span, 'head', axis=1, tiled=True)  51.9 us
    all_to_all x1, waiting for transfers between devices, several_exchanges(): lax.all_to_all(share, axis, split_axis=0, concat_axis=0, tiled=True)  51 us
    sub x1, matrix products, attend_block(): weights = jnp.where(live, jnp.exp(scores - top[..., None]), 0.0)  17.6 us
    dot_general x1, matrix products, per_device(): lax.dot_general(lax.all_gather(mine_cols, 'doc', axis=0, tiled=True), col...  12.6 us
  transfers between devices with their start and end apart: 5, of which 3 were waited for; matrix products, arithmetic and copies ran while one was open for 13% of the time, Pallas kernels for 0%

commit v1 on v0

--- a/solution.py
+++ b/solution.py
@@ -133,7 +133,9 @@
         doc_count * tok_rows * ctx_count, slice_width
     )
     product = lax.dot_general(
-        lax.all_gather(mine_cols, "doc", axis=0, tiled=True),
+        jnp.concatenate(
+            lax.all_to_all(jnp.stack([mine_cols] * lax.axis_size("doc")), "doc", 0, 0), axis=0
+        ),
         column_set,
         (((0,), (0,)), ((), ())),
         preferred_element_type=jnp.float32,

time: 353 us -> 661 us (1.87)
  the two profiles are of different devices: /device:TPU:8 before, /device:TPU:120 now
where the time goes in v1:
time: 661 us; the launch traced here: 660 us
  waiting for transfers between devices  481 us (73%)
  blocking collectives  62.3 us (9%)
  matrix products  37.1 us (6%)
  local copies, waits for them, and re-layouts  33.7 us (5%)
  starting transfers between devices  25.4 us (4%)
  between operations  14.2 us (2%)
    all_to_all x1, waiting for transfers between devices, per_device(): lax.all_to_all(jnp.stack([mine_cols] * lax.axis_size('doc')), 'doc', 0, 0)  382 us
    all_to_all x1, blocking collectives, several_exchanges(): lax.all_to_all(share, axis, split_axis=0, concat_axis=0, tiled=True)  57.7 us
    all_gather x1, waiting for transfers between devices, per_device(): full_doc = lax.all_gather(span, 'head', axis=1, tiled=True)  52.6 us
    all_to_all x1, waiting for transfers between devices, several_exchanges(): lax.all_to_all(share, axis, split_axis=0, concat_axis=0, tiled=True)  46.2 us
    sub x1, matrix products, attend_block(): weights = jnp.where(live, jnp.exp(scores - top[..., None]), 0.0)  17.6 us
  transfers between devices with their start and end apart: 5, of which 3 were waited for; matrix products, arithmetic and copies ran while one was open for 6% of the time, Pallas kernels for 0%

profile of v1, /device:TPU:120, one launch (start us, length us, event | category | flops | bytes accessed | tf_op | source)
XLA Modules:
  0.0 659.8 jit_solution(3869038775427689752)
XLA Ops:
  9.0 1.5 gather_fusion.2
  10.9 1.9 gather_fusion.1
  12.8 3.7 all-to-all-start.1
  17.1 3.4 gather_fusion
  20.5 4.6 all-to-all-start
  25.2 1.8 reshape.231
  27.1 17.6 %fusion.33 = (f32[2,8,128]{2,1,0:T(8,128)S(1)}, bf16[2,8,128,3072]{2,3,1,0:T(8,128)(2,1)}) fusion(pred[3072]{0:T(1024)(128)(4,1)S(1)} %broadcast_bitcast_fusion, bf16[3072,2,128,1]{2,1,0,3:T(2,128)(2,1)} %bitcast.85, bf16[128,2,8,128]{3,2,1,0:T(8,128)(2,1)S(1)} %bitcast.88), kind=kOutput, calls=%fused_computation.58 | convolution fusion | flops 1648364544 | bytes 14691328 | tf_op jit(solution)/shard_map/while/body/eval_jaxpr/sub | solution.py:75
  44.6 3.5 reshape.228
  48.2 7.0 %fusion.6 = f32[2,128,8,128]{3,1,2,0:T(8,128)S(1)} fusion(bf16[2,8,128,3072]{2,3,1,0:T(8,128)(2,1)} %get-tuple-element.28, bf16[3072,2,128,1]{2,1,0,3:T(2,128)(2,1)} %bitcast.83), kind=kOutput, calls=%fused_computation.10 | convolution fusion | flops 1610612736 | bytes 15204352 | tf_op jit(solution)/shard_map/while/body/eval_jaxpr/kgqs,skd->qkgd/dot_general | solution.py:77
  55.3 4.6 all_to_all.30
  59.9 1.1 copy_bitcast_fusion
  61.0 52.6 %all-gather.2.cloned.1.call-done = bf16[256,8192]{0,1:T(8,128)(2,1)} async-done(((bf16[256,2048]{0,1:T(8,128)(2,1)}), bf16[256,8192]{0,1:T(8,128)(2,1)}) %all-gather.2.cloned.1.call-update) | async-done | bytes 4194320 | tf_op jit(solution)/shard_map/all_gather | solution.py:129
  113.6 4.0 slice_bitcast_fusion.1
  117.6 57.7 %all_to_all.31 = bf16[32,128,1,256]{1,3,2,0:T(8,128)(2,1)} all-to-all(bf16[32,128,1,256]{1,3,2,0:T(8,128)(2,1)S(1)} %get-tuple-element.19), channel_id=1, replica_groups=mesh['ctx'=2,'head'=4,'doc'=32] {'doc'}, dimensions={0} | all-to-all | bytes 4194304 | tf_op jit(solution)/shard_map/all_to_all | solution.py:51
  175.3 8.3 %all-to-all-start.4 = ((bf16[32,128,1,256]{1,3,2,0:T(8,128)(2,1)}), bf16[32,128,1,256]{1,3,2,0:T(8,128)(2,1)}, u32[]{:S(2)}, u32[]{:S(2)}) async-start(bf16[32,128,1,256]{1,3,2,0:T(8,128)(2,1)} %get-tuple-element.18), calls=%async_computation.4 | async-start | bytes 4194304 | tf_op jit(solution)/shard_map/all_to_all | solution.py:51
  183.9 46.2 %all-to-all-done.4 = bf16[32,128,1,256]{1,3,2,0:T(8,128)(2,1)} async-done(((bf16[32,128,1,256]{1,3,2,0:T(8,128)(2,1)}), bf16[32,128,1,256]{1,3,2,0:T(8,128)(2,1)}, u32[]{:S(2)}, u32[]{:S(2)}) %all-to-all-start.4) | async-done | bytes 2097184 | tf_op jit(solution)/shard_map/all_to_all | solution.py:51
  230.1 5.9 stack.2
  236.0 8.7 %all-to-all-start.3 = ((bf16[32,256,1024]{2,1,0:T(8,128)(2,1)}), bf16[32,256,1024]{2,1,0:T(8,128)(2,1)}, u32[]{:S(2)}, u32[]{:S(2)}) async-start(bf16[32,256,1024]{2,1,0:T(8,128)(2,1)} %stack.2), calls=%async_computation.3 | async-start | bytes 33554432 | tf_op jit(solution)/shard_map/all_to_all | solution.py:137
  245.7 0.9 divide_convert_fusion
  246.6 3.3 copy.84
  249.9 4.1 copy.83
  253.9 4.1 pad_maximum_fusion
  258.0 382.3 %all-to-all-done.3 = bf16[32,256,1024]{2,1,0:T(8,128)(2,1)} async-done(((bf16[32,256,1024]{2,1,0:T(8,128)(2,1)}), bf16[32,256,1024]{2,1,0:T(8,128)(2,1)}, u32[]{:S(2)}, u32[]{:S(2)}) %all-to-all-start.3) | async-done | bytes 16777248 | tf_op jit(solution)/shard_map/all_to_all | solution.py:137
  640.4 12.6 %fusion.42 = f32[1024,256]{1,0:T(8,128)} fusion(bf16[8192,1024]{1,0:T(8,128)(2,1)} %bitcast.18, bf16[8192,256]{1,0:T(8,128)(2,1)} %bitcast.79), kind=kOutput, calls=%fused_computation.59 | convolution fusion | flops 4294967296 | bytes 22020096 | tf_op jit(solution)/shard_map/dot_general | solution.py:135
  (45 shorter events, 4.2 us)
Async XLA Ops:
  7.2 3.8 copy-start
  7.2 9.4 %copy-start.2 = (s32[1,2,16]{2,1,0:T(2,128)S(1)}, s32[1,2,16]{2,1,0:T(2,128)}, u32[]{:S(2)}) copy-start(s32[1,2,16]{2,1,0:T(2,128)} %param.7) | copy-start | bytes 388
  7.2 9.8 %copy-start.4 = (bf16[1,128,2048]{2,1,0:T(8,128)(2,1)S(1)}, bf16[1,128,2048]{2,1,0:T(8,128)(2,1)}, u32[]{:S(2)}) copy-start(bf16[1,128,2048]{2,1,0:T(8,128)(2,1)} %param.4) | copy-start | bytes 1572868
  12.8 7.7 %all-to-all-start.1 = ((bf16[2,1,12,128,256]{4,3,2,1,0:T(8,128)(2,1)}), bf16[2,1,12,128,256]{4,3,2,1,0:T(8,128)(2,1)S(1)}, u32[]{:S(2)}, u32[]{:S(2)}) async-start(bf16[2,1,12,128,256]{4,3,2,1,0:T(8,128)(2,1)} %bitcast.81), calls=%async_computation.1 | async-start | bytes 3145728 | tf_op jit(solution)/shard_map/all_to_all | solution.py:104
  20.5 24.1 %all-to-all-start = ((bf16[2,1,12,128,256]{4,3,2,1,0:T(8,128)(2,1)}), bf16[2,1,12,128,256]{4,3,2,1,0:T(8,128)(2,1)}, u32[]{:S(2)}, u32[]{:S(2)}) async-start(bf16[2,1,12,128,256]{4,3,2,1,0:T(8,128)(2,1)} %bitcast.82), calls=%async_computation | async-start | bytes 3145728 | tf_op jit(solution)/shard_map/all_to_all | solution.py:105
  25.2 88.4 %all-gather.2.cloned.1.call-start = ((), (), s32[]{:S(2)}) async-start(), calls=%async_computation.6 | async-start | bytes 5242880 | tf_op jit(solution)/shard_map/all_gather | solution.py:129
  117.6 66.0 %copy-start.3 = (bf16[256,2048]{0,1:T(8,128)(2,1)S(1)}, bf16[256,2048]{0,1:T(8,128)(2,1)}, u32[]{:S(2)}) copy-start(bf16[256,2048]{0,1:T(8,128)(2,1)} %copy_bitcast_fusion) | copy-start | bytes 3145732
  175.3 54.8 %all-to-all-start.4 = ((bf16[32,128,1,256]{1,3,2,0:T(8,128)(2,1)}), bf16[32,128,1,256]{1,3,2,0:T(8,128)(2,1)}, u32[]{:S(2)}, u32[]{:S(2)}) async-start(bf16[32,128,1,256]{1,3,2,0:T(8,128)(2,1)} %get-tuple-element.18), calls=%async_computation.4 | async-start | bytes 4194304 | tf_op jit(solution)/shard_map/all_to_all | solution.py:51
  236.0 404.3 %all-to-all-start.3 = ((bf16[32,256,1024]{2,1,0:T(8,128)(2,1)}), bf16[32,256,1024]{2,1,0:T(8,128)(2,1)}, u32[]{:S(2)}, u32[]{:S(2)}) async-start(bf16[32,256,1024]{2,1,0:T(8,128)(2,1)} %stack.2), calls=%async_computation.3 | async-start | bytes 33554432 | tf_op jit(solution)/shard_map/all_to_all | solution.py:137
  640.3 12.6 %copy-start.1 = (bf16[1,4096,256]{2,1,0:T(8,128)(2,1)S(1)}, bf16[1,4096,256]{2,1,0:T(8,128)(2,1)}, u32[]{:S(2)}) copy-start(bf16[1,4096,256]{2,1,0:T(8,128)(2,1)} %param.5) | copy-start | bytes 6291460
Sparse Core Ops, SparseCore 0:
  61.1 52.4 all-gather.1
